TPU v7x, 32 devices: a whole 2x2x4 slice. The times are simulated.
32 devices in a mesh: tensor: 8 (over z, core), example: 4 (over y, x).
Axes of the slice: x: 2, y: 2, z: 4, core: 2. Of those that a mesh axis runs over, the one named last changes fastest.
Arguments:
- acts: bfloat16 [256, 8192], P(None, 'example'), may hold values from -6 to 6
- out_grad: bfloat16 [256, 8192], P(None, 'example'), may hold values from -6 to 6
- w_gate: bfloat16 [8192, 28672], P('example', 'tensor'), may hold values from -0.0625 to 0.0625
- w_up: bfloat16 [8192, 28672], P('example', 'tensor'), may hold values from -0.0625 to 0.0625
- w_down: bfloat16 [28672, 8192], P('tensor', 'example'), may hold values from -0.03125 to 0.03125
- proj_in: bfloat16 [8192, 64], P('example'), may hold values from -0.0625 to 0.0625
- proj_gate: bfloat16 [28672, 64], P('tensor'), may hold values from -0.03125 to 0.03125
- proj_up: bfloat16 [28672, 64], P('tensor'), may hold values from -0.03125 to 0.03125
- proj_hidden: bfloat16 [28672, 64], P('tensor'), may hold values from -0.03125 to 0.03125
- proj_out: bfloat16 [8192, 64], P('example'), may hold values from -0.0625 to 0.0625
- store: bfloat16 [4096, 12288], P(('tensor', 'example')), may hold values from -0.0546875 to 0.0546875
- doc_ids: int32 [32, 128], P(('tensor', 'example')), may hold values from 0 to 127, each once within a row
Outputs:
- scores: float32 [4, 4096], P(None, ('tensor', 'example'))
Inputs may be any that keep to these rules, and one draw needn't show every extreme that they name: Each row of doc_ids is a permutation of 0 to 127.
All inputs are finite; a program needn't handle non-finite values.
Results may differ from a plain program's by a relative error of at most 0.022.
Values may be sent and summed in bfloat16 or wider, within the bound.
No kernel may reach another device: no remote copies, remote signals or barrier semaphores. Data moves between devices by JAX's collectives and lax.ppermute only.
A program may use at most 128 MiB of HBM per device.

v0:
```python
import jax
import jax.numpy as jnp
from jax import lax
from jax.sharding import PartitionSpec as P

SEQ_LEN = 64


def grads_of(gate, up, grad_hidden):
    sig = jax.nn.sigmoid(gate)
    hidden = gate * sig * up
    grad_up = grad_hidden * gate * sig
    grad_gate = grad_hidden * up * sig * (1.0 + gate * (1.0 - sig))
    return (
        hidden.astype(jnp.bfloat16),
        grad_gate.astype(jnp.bfloat16),
        grad_up.astype(jnp.bfloat16),
    )


def outer_sums(left, right):
    count = left.shape[0] // SEQ_LEN
    left_seq = left.reshape(count, SEQ_LEN, left.shape[1])
    right_seq = right.reshape(count, SEQ_LEN, right.shape[1])
    total = jnp.einsum("stq,str->sqr", left_seq, right_seq, precision=lax.Precision.HIGHEST)
    return total.reshape(count, left.shape[1] * right.shape[1])


def query_of(in_proj, gate_proj, up_proj, hidden_proj, out_proj):
    return jnp.concatenate(
        [
            outer_sums(in_proj, gate_proj),
            outer_sums(in_proj, up_proj),
            outer_sums(hidden_proj, out_proj),
        ],
        axis=1,
    )


def local(
    acts,
    out_grad,
    w_gate,
    w_up,
    w_down,
    proj_in,
    proj_gate,
    proj_up,
    proj_hidden,
    proj_out,
    store,
    doc_ids,
):
    width = w_gate.shape[1]
    rank = proj_in.shape[1]
    contract_last = (((1,), (1,)), ((), ()))
    left_weights = jnp.concatenate([w_gate, w_up, proj_in], axis=1)
    forward = jnp.dot(acts, left_weights, preferred_element_type=jnp.float32)
    backward = lax.dot_general(out_grad, w_down, contract_last, preferred_element_type=jnp.float32)
    outward = jnp.dot(out_grad, proj_out, preferred_element_type=jnp.float32)
    summed = lax.psum_scatter(
        jnp.concatenate([forward, backward, outward], axis=1).astype(jnp.bfloat16),
        "example",
        scatter_dimension=0,
        tiled=True,
    ).astype(jnp.float32)
    gate = summed[:, :width]
    up = summed[:, width : 2 * width]
    in_proj = summed[:, 2 * width : 2 * width + rank]
    grad_hidden = summed[:, 2 * width + rank : 3 * width + rank]
    out_proj = summed[:, 3 * width + rank :]
    hidden, grad_gate, grad_up = grads_of(gate, up, grad_hidden)
    gate_part = jnp.dot(grad_gate, proj_gate, preferred_element_type=jnp.float32)
    up_part = jnp.dot(grad_up, proj_up, preferred_element_type=jnp.float32)
    hidden_part = jnp.dot(hidden, proj_hidden, preferred_element_type=jnp.float32)
    gate_proj, up_proj, hidden_proj = (
        lax.psum(gate_part.astype(jnp.bfloat16), "tensor").astype(jnp.float32),
        lax.psum(up_part.astype(jnp.bfloat16), "tensor").astype(jnp.float32),
        lax.psum(hidden_part.astype(jnp.bfloat16), "tensor").astype(jnp.float32),
    )
    own_query = query_of(in_proj, gate_proj, up_proj, hidden_proj, out_proj).astype(jnp.bfloat16)
    query = lax.all_gather(own_query, "example", axis=0, tiled=True)
    picked = jnp.take(store, doc_ids[0], axis=0)
    return lax.dot_general(query, picked, contract_last, preferred_element_type=jnp.float32)


def solution(mesh):
    return jax.shard_map(
        local,
        mesh=mesh,
        in_specs=(
            P(None, "example"),
            P(None, "example"),
            P("example", "tensor"),
            P("example", "tensor"),
            P("tensor", "example"),
            P("example", None),
            P("tensor", None),
            P("tensor", None),
            P("tensor", None),
            P("example", None),
            P(("tensor", "example"), None),
            P(("tensor", "example"), None),
        ),
        out_specs=P(None, ("tensor", "example")),
        check_vma=False,
    )
```

profile of v0, /device:TPU:0, one launch (start us, length us, event | category | flops | bytes accessed | tf_op | source)
XLA Modules:
  0.0 193.3 jit_solution(8513815710191261834)
XLA Ops:
  6.5 0.0 copy-start
  6.5 0.0 reduce-scatter.4.cloned.1.call-start
  6.5 2.1 %copy.17 = bf16[2048,64]{1,0:T(8,128)(2,1)} copy(bf16[2048,64]{0,1:T(8,128)(2,1)} %param.17) | data formatting | bytes 524288 | tf_op args[5]
  8.7 9.7 %convolution_convert_fusion = bf16[256,3584]{0,1:T(8,128)(2,1)S(1)} fusion(bf16[256,2048]{1,0:T(8,128)(2,1)} %param.13, bf16[3584,2048]{1,0:T(8,128)(2,1)} %param.16), kind=kOutput, calls=%fused_computation.10 | convolution fusion | flops 3759013888 | bytes 17563648 | tf_op jit(solution)/shard_map/dot_general | solution.py:59
  18.3 0.0 copy-done.1
  18.3 0.0 copy-done.3
  18.3 0.4 convolution_convert_fusion.1
  18.8 14.2 %fusion.9 = bf16[256,7232]{0,1:T(8,128)(2,1)S(1)} fusion(bf16[256,2048]{1,0:T(8,128)(2,1)S(1)} %copy-done.4, bf16[2048,64]{1,0:T(8,128)(2,1)S(1)} %copy-done.2, bf16[2048,3584]{1,0:T(8,128)(2,1)} %param.15, bf16[2048,3584]{1,0:T(8,128)(2,1)} %param.14), kind=kOutput, calls=%fused_computation.8 | convolution fusion | flops 7674019840 | bytes 34373632 | tf_op jit(solution)/shard_map/dot_general | solution.py:58
  33.0 25.2 %pad_maximum_fusion = bf16[256,10880]{0,1:T(8,128)(2,1)} fusion(bf16[256,64]{0,1:T(8,128)(2,1)S(1)} %convolution_convert_fusion.1, bf16[256,3584]{0,1:T(8,128)(2,1)S(1)} %convolution_convert_fusion, bf16[256,7232]{0,1:T(8,128)(2,1)S(1)} %fusion.9), kind=kLoop, calls=%fused_computation.9 | loop fusion | flops 16711680 | bytes 11141120 | tf_op jit(solution)/shard_map/concatenate | solution.py:62
  58.2 8.3 %copy.20 = bf16[256,10880]{1,0:T(8,128)(2,1)} copy(bf16[256,10880]{0,1:T(8,128)(2,1)} %pad_maximum_fusion) | data formatting | bytes 11141120
  66.5 0.0 reduce-scatter.4.cloned.1.call-update
  66.5 0.6 copy-done.8
  67.2 4.2 %gather_fusion = bf16[128,12288]{1,0:T(8,128)(2,1)} fusion(bf16[128,12288]{1,0:T(8,128)(2,1)S(1)} %copy-done, s32[1024]{0:T(1024)S(1)} %pad_clamp_fusion), kind=kCustom, calls=%fused_computation | custom fusion | bytes 6291968 | tf_op jit(solution)/shard_map/jit(_take)/gather | solution.py:83
  71.4 62.1 %reduce-scatter.4.cloned.1.call-done = bf16[64,10880]{1,0:T(8,128)(2,1)} async-done(((bf16[256,10880]{1,0:T(8,128)(2,1)}), bf16[64,10880]{1,0:T(8,128)(2,1)}) %reduce-scatter.4.cloned.1.call-update) | async-done | bytes 1392656
  133.5 4.0 %copy.21 = bf16[64,10880]{0,1:T(8,128)(2,1)} copy(bf16[64,10880]{1,0:T(8,128)(2,1)} %reduce-scatter.4.cloned.1.call-done) | data formatting | bytes 2785280
  137.5 2.0 %convert_element_type.34 = f32[64,10880]{0,1:T(8,128)S(1)} convert(bf16[64,10880]{0,1:T(8,128)(2,1)} %copy.21) | non-fusion elementwise | flops 696320 | bytes 4177920 | tf_op jit(solution)/shard_map/convert_element_type | solution.py:66
  139.6 0.0 copy-start.6
  139.6 0.7 convolution_convert_fusion.2
  140.3 0.3 copy-done.6
  140.6 0.7 convolution_convert_fusion.3
  141.3 0.3 copy-done.7
  141.6 0.9 convolution_convert_fusion.4
  142.5 29.0 %all-reduce = (bf16[64,64]{1,0:T(8,128)(2,1)S(1)}, bf16[64,64]{1,0:T(8,128)(2,1)S(1)}, bf16[64,64]{1,0:T(8,128)(2,1)S(1)}) all-reduce(bf16[64,64]{1,0:T(8,128)(2,1)S(1)} %convolution_convert_fusion.2, bf16[64,64]{1,0:T(8,128)(2,1)S(1)} %convolution_convert_fusion.3, ...), channel_id=1, replica_groups=mesh['tensor'=8,'example'=4] {'tensor'}, use_global_device_ids=true, to_apply=%region_3.0 | all-reduce | flops 12288 | bytes 49152 | tf_op jit(solution)/shard_map/psum | solution.py:79
  171.5 0.8 convolution_convert_fusion.7
  172.4 0.1 concatenate.27
  172.5 0.8 convolution_convert_fusion.6
  173.3 0.1 concatenate.28
  173.4 0.9 convolution_convert_fusion.5
  174.3 0.1 concatenate.29
  174.4 0.1 maximum_bitcast_fusion
  174.5 8.5 %all-gather = bf16[4,1,12288]{2,1,0:T(2,128)(2,1)S(1)} all-gather(bf16[1,1,12288]{2,1,0:T(2,128)(2,1)S(1)} %maximum_bitcast_fusion), channel_id=1, replica_groups=mesh['tensor'=8,'example'=4] {'example'}, dimensions={0}, use_global_device_ids=true | all-gather | bytes 122880 | tf_op jit(solution)/shard_map/all_gather | solution.py:82
  183.0 3.5 %fusion.12 = f32[4,128]{1,0:T(4,128)} fusion(bf16[128,12288]{1,0:T(8,128)(2,1)} %gather_fusion, pred[128]{0:T(512)(128)(4,1)S(1)} %compare_and_fusion, bf16[4,1,12288]{2,1,0:T(2,128)(2,1)S(1)} %all-gather), kind=kOutput, calls=%fused_computation.11 | convolution fusion | flops 14155776 | bytes 3246208 | tf_op jit(solution)/shard_map/dot_general | solution.py:84
  (14 shorter events, 0.0 us)
Async XLA Ops:
  6.5 60.6 %copy-start = (bf16[128,12288]{1,0:T(8,128)(2,1)S(1)}, bf16[128,12288]{1,0:T(8,128)(2,1)}, u32[]{:S(2)}) copy-start(bf16[128,12288]{1,0:T(8,128)(2,1)} %param.22) | copy-start | bytes 9437188
  6.5 127.0 %reduce-scatter.4.cloned.1.call-start = ((), (), s32[]{:S(2)}) async-start(), calls=%async_computation.1 | async-start | bytes 6963200
  8.6 9.7 %copy-start.1 = (bf16[256,2048]{1,0:T(8,128)(2,1)S(1)}, bf16[256,2048]{1,0:T(8,128)(2,1)}, u32[]{:S(2)}) copy-start(bf16[256,2048]{1,0:T(8,128)(2,1)} %param.13) | copy-start | bytes 3145732
  8.6 9.7 %copy-start.3 = (bf16[2048,64]{0,1:T(8,128)(2,1)S(1)}, bf16[2048,64]{0,1:T(8,128)(2,1)}, u32[]{:S(2)}) copy-start(bf16[2048,64]{0,1:T(8,128)(2,1)} %param.21) | copy-start | bytes 786436
  8.6 10.1 %copy-start.2 = (bf16[2048,64]{1,0:T(8,128)(2,1)S(1)}, bf16[2048,64]{1,0:T(8,128)(2,1)}, u32[]{:S(2)}) copy-start(bf16[2048,64]{1,0:T(8,128)(2,1)} %copy.17) | copy-start | bytes 786436
  8.6 10.2 %copy-start.4 = (bf16[256,2048]{1,0:T(8,128)(2,1)S(1)}, bf16[256,2048]{1,0:T(8,128)(2,1)}, u32[]{:S(2)}) copy-start(bf16[256,2048]{1,0:T(8,128)(2,1)} %param.12) | copy-start | bytes 3145732
  66.5 0.7 copy-start.8
  137.5 2.0 %copy-start.5 = (bf16[3584,64]{0,1:T(8,128)(2,1)S(1)}, bf16[3584,64]{0,1:T(8,128)(2,1)}, u32[]{:S(2)}) copy-start(bf16[3584,64]{0,1:T(8,128)(2,1)} %param.20) | copy-start | bytes 1376260
  139.6 1.0 copy-start.6
  140.6 1.0 copy-start.7
Sparse Core Ops, SparseCore 0:
  66.6 66.8 reduce-scatter.3
where the time goes:
time: 194 us; the launch traced here: 193 us
  waiting for transfers between devices  62.2 us (32%)
  blocking collectives  37.6 us (19%)
  matrix products  32.7 us (17%)
  other arithmetic  27.3 us (14%)
  local copies, waits for them, and re-layouts  20.1 us (10%)
  between operations  13.5 us (7%)
    unnamed x2, waiting for transfers between devices  62.2 us
    psum x1, blocking collectives, local(): lax.psum(hidden_part.astype(jnp.bfloat16), 'tensor').astype(jnp.float32)  29 us
    concatenate x1, other arithmetic, local(): jnp.concatenate([forward, backward, outward], axis=1).astype(jnp.bfloat16)  25.2 us
    unnamed x21, local copies, waits for them, and re-layouts  15.6 us
    dot_general x1, matrix products, local(): forward = jnp.dot(acts, left_weights, preferred_element_type=jnp.float32)  14.2 us
    dot_general x1, matrix products, local(): lax.dot_general(out_grad, w_down, contract_last, preferred_element_type=j...  9.66 us
    all_gather x1, blocking collectives, local(): query = lax.all_gather(own_query, 'example', axis=0, tiled=True)  8.53 us
    gather x1, local copies, waits for them, and re-layouts, local(): picked = jnp.take(store, doc_ids[0], axis=0)  4.22 us
  transfers between devices with their start and end apart: 1, of which 1 were waited for; matrix products, arithmetic and copies ran while one was open for 2% of the time, Pallas kernels for 0%

commit v1 on v0

--- a/solution.py
+++ b/solution.py
@@ -76,7 +76,9 @@
     gate_proj, up_proj, hidden_proj = (
         lax.psum(gate_part.astype(jnp.bfloat16), "tensor").astype(jnp.float32),
         lax.psum(up_part.astype(jnp.bfloat16), "tensor").astype(jnp.float32),
-        lax.psum(hidden_part.astype(jnp.bfloat16), "tensor").astype(jnp.float32),
+        jnp.sum(lax.all_gather(hidden_part.astype(jnp.bfloat16), "tensor"), axis=0).astype(
+            jnp.float32
+        ),
     )
     own_query = query_of(in_proj, gate_proj, up_proj, hidden_proj, out_proj).astype(jnp.bfloat16)
     query = lax.all_gather(own_query, "example", axis=0, tiled=True)

time: 194 us -> 211 us (1.088)
  blocking collectives: 37.6 us -> 51.1 us
    all_gather x0 -> x1, blocking collectives: none -> 14 us  [local(): lax.all_gather(hidden_part.astype(jnp.bfloat16), 'tensor')]
    dot_general x1, matrix products: 0.72 us -> 2.85 us  [local(): jnp.dot(hidden, proj_hidden, preferred_element_type=jnp.float32)]
where the time goes in v1:
time: 211 us; the launch traced here: 210 us
  waiting for transfers between devices  62.2 us (29%)
  blocking collectives  51.1 us (24%)
  matrix products  34.8 us (16%)
  other arithmetic  27.4 us (13%)
  local copies, waits for them, and re-layouts  21.3 us (10%)
  between operations  13.5 us (6%)
    unnamed x2, waiting for transfers between devices  62.2 us
    psum x1, blocking collectives, local(): lax.psum(up_part.astype(jnp.bfloat16), 'tensor').astype(jnp.float32)  28.6 us
    concatenate x1, other arithmetic, local(): jnp.concatenate([forward, backward, outward], axis=1).astype(jnp.bfloat16)  25.2 us
    unnamed x21, local copies, waits for them, and re-layouts  16.8 us
    dot_general x1, matrix products, local(): forward = jnp.dot(acts, left_weights, preferred_element_type=jnp.float32)  14.2 us
    all_gather x1, blocking collectives, local(): lax.all_gather(hidden_part.astype(jnp.bfloat16), 'tensor')  14 us
    dot_general x1, matrix products, local(): lax.dot_general(out_grad, w_down, contract_last, preferred_element_type=j...  9.66 us
    all_gather x1, blocking collectives, local(): query = lax.all_gather(own_query, 'example', axis=0, tiled=True)  8.55 us
  transfers between devices with their start and end apart: 1, of which 1 were waited for; matrix products, arithmetic and copies ran while one was open for 2% of the time, Pallas kernels for 0%

profile of v1, /device:TPU:0, one launch (start us, length us, event | category | flops | bytes accessed | tf_op | source)
XLA Modules:
  0.0 210.2 jit_solution(4972413996696922291)
XLA Ops:
  6.5 0.0 reduce-scatter.4.cloned.1.call-start
  6.5 2.1 %copy.17 = bf16[2048,64]{1,0:T(8,128)(2,1)} copy(bf16[2048,64]{0,1:T(8,128)(2,1)} %param.17) | data formatting | bytes 524288 | tf_op args[5]
  8.7 9.7 %convolution_convert_fusion = bf16[256,3584]{0,1:T(8,128)(2,1)S(1)} fusion(bf16[256,2048]{1,0:T(8,128)(2,1)} %param.13, bf16[3584,2048]{1,0:T(8,128)(2,1)} %param.16), kind=kOutput, calls=%fused_computation.10 | convolution fusion | flops 3759013888 | bytes 17563648 | tf_op jit(solution)/shard_map/dot_general | solution.py:59
  18.3 0.0 copy-done.2
  18.3 0.0 copy-done.4
  18.3 0.4 convolution_convert_fusion.1
  18.8 0.0 copy-done.5
  18.8 14.2 %fusion.9 = bf16[256,7232]{0,1:T(8,128)(2,1)S(1)} fusion(bf16[256,2048]{1,0:T(8,128)(2,1)S(1)} %copy-done.5, bf16[2048,64]{1,0:T(8,128)(2,1)S(1)} %copy-done.3, bf16[2048,3584]{1,0:T(8,128)(2,1)} %param.15, bf16[2048,3584]{1,0:T(8,128)(2,1)} %param.14), kind=kOutput, calls=%fused_computation.8 | convolution fusion | flops 7674019840 | bytes 34373632 | tf_op jit(solution)/shard_map/dot_general | solution.py:58
  33.0 25.2 %pad_maximum_fusion = bf16[256,10880]{0,1:T(8,128)(2,1)} fusion(bf16[256,64]{0,1:T(8,128)(2,1)S(1)} %convolution_convert_fusion.1, bf16[256,3584]{0,1:T(8,128)(2,1)S(1)} %convolution_convert_fusion, bf16[256,7232]{0,1:T(8,128)(2,1)S(1)} %fusion.9), kind=kLoop, calls=%fused_computation.9 | loop fusion | flops 16711680 | bytes 11141120 | tf_op jit(solution)/shard_map/concatenate | solution.py:62
  58.3 8.3 %copy.20 = bf16[256,10880]{1,0:T(8,128)(2,1)} copy(bf16[256,10880]{0,1:T(8,128)(2,1)} %pad_maximum_fusion) | data formatting | bytes 11141120
  66.6 0.0 reduce-scatter.4.cloned.1.call-update
  66.6 0.6 copy-done.8
  67.3 4.2 %gather_fusion = bf16[128,12288]{1,0:T(8,128)(2,1)} fusion(bf16[128,12288]{1,0:T(8,128)(2,1)S(1)} %copy-done, s32[1024]{0:T(1024)S(1)} %pad_clamp_fusion), kind=kCustom, calls=%fused_computation | custom fusion | bytes 6291968 | tf_op jit(solution)/shard_map/jit(_take)/gather | solution.py:85
  71.5 62.2 %reduce-scatter.4.cloned.1.call-done = bf16[64,10880]{1,0:T(8,128)(2,1)} async-done(((bf16[256,10880]{1,0:T(8,128)(2,1)}), bf16[64,10880]{1,0:T(8,128)(2,1)}) %reduce-scatter.4.cloned.1.call-update) | async-done | bytes 1392656
  133.6 4.0 %copy.21 = bf16[64,10880]{0,1:T(8,128)(2,1)} copy(bf16[64,10880]{1,0:T(8,128)(2,1)} %reduce-scatter.4.cloned.1.call-done) | data formatting | bytes 2785280
  137.6 2.0 convert_element_type.36
  139.7 0.0 copy-start.7
  139.7 0.7 convolution_convert_fusion.3
  140.4 1.7 copy-done.1
  142.1 0.9 convolution_convert_fusion.4
  143.0 28.6 %all-reduce = (bf16[64,64]{1,0:T(8,128)(2,1)S(1)}, bf16[64,64]{1,0:T(8,128)(2,1)S(1)}) all-reduce(bf16[64,64]{1,0:T(8,128)(2,1)S(1)} %convolution_convert_fusion.3, bf16[64,64]{1,0:T(8,128)(2,1)S(1)} %convolution_convert_fusion.4), channel_id=1, replica_groups=mesh['tensor'=8,'example'=4] {'tensor'}, use_global_device_ids=true, to_apply=%region_2.0 | all-reduce | flops 8192 | bytes 32768 | tf_op jit(solution)/shard_map/psum | solution.py:78
  171.6 0.8 convolution_convert_fusion.7
  172.4 0.1 concatenate.27
  172.5 0.8 convolution_convert_fusion.6
  173.4 0.1 concatenate.28
  173.5 2.8 %convolution_convert_fusion.2 = bf16[64,64]{1,0:T(8,128)(2,1)S(1)} fusion(bf16[3584,64]{0,1:T(8,128)(2,1)} %param.20, f32[64,10880]{0,1:T(8,128)} %copy-done.1), kind=kOutput, calls=%fused_computation.20 | convolution fusion | flops 30740480 | bytes 4136960 | tf_op jit(solution)/shard_map/dot_general | solution.py:75
  176.3 14.0 %all-gather = bf16[512,64]{1,0:T(8,128)(2,1)S(1)} all-gather(bf16[64,64]{1,0:T(8,128)(2,1)S(1)} %convolution_convert_fusion.2), channel_id=2, replica_groups=mesh['tensor'=8,'example'=4] {'tensor'}, dimensions={0}, use_global_device_ids=true | all-gather | bytes 73728 | tf_op jit(solution)/shard_map/all_gather | solution.py:79
  190.3 0.9 convolution_convert_fusion.5
  191.2 0.1 concatenate.29
  191.3 0.1 maximum_bitcast_fusion
  191.3 8.5 %all-gather.1 = bf16[4,1,12288]{2,1,0:T(2,128)(2,1)S(1)} all-gather(bf16[1,1,12288]{2,1,0:T(2,128)(2,1)S(1)} %maximum_bitcast_fusion), channel_id=1, replica_groups=mesh['tensor'=8,'example'=4] {'example'}, dimensions={0}, use_global_device_ids=true | all-gather | bytes 122880 | tf_op jit(solution)/shard_map/all_gather | solution.py:84
  199.9 3.5 %fusion.12 = f32[4,128]{1,0:T(4,128)} fusion(bf16[128,12288]{1,0:T(8,128)(2,1)} %gather_fusion, pred[128]{0:T(512)(128)(4,1)S(1)} %compare_and_fusion, bf16[4,1,12288]{2,1,0:T(2,128)(2,1)S(1)} %all-gather.1), kind=kOutput, calls=%fused_computation.11 | convolution fusion | flops 14155776 | bytes 3246208 | tf_op jit(solution)/shard_map/dot_general | solution.py:86
  (16 shorter events, 0.1 us)
Async XLA Ops:
  6.5 60.7 %copy-start = (bf16[128,12288]{1,0:T(8,128)(2,1)S(1)}, bf16[128,12288]{1,0:T(8,128)(2,1)}, u32[]{:S(2)}) copy-start(bf16[128,12288]{1,0:T(8,128)(2,1)} %param.22) | copy-start | bytes 9437188
  6.5 127.1 %reduce-scatter.4.cloned.1.call-start = ((), (), s32[]{:S(2)}) async-start(), calls=%async_computation.1 | async-start | bytes 6963200
  8.6 9.7 %copy-start.2 = (bf16[256,2048]{1,0:T(8,128)(2,1)S(1)}, bf16[256,2048]{1,0:T(8,128)(2,1)}, u32[]{:S(2)}) copy-start(bf16[256,2048]{1,0:T(8,128)(2,1)} %param.13) | copy-start | bytes 3145732
  8.6 9.7 %copy-start.4 = (bf16[2048,64]{0,1:T(8,128)(2,1)S(1)}, bf16[2048,64]{0,1:T(8,128)(2,1)}, u32[]{:S(2)}) copy-start(bf16[2048,64]{0,1:T(8,128)(2,1)} %param.21) | copy-start | bytes 786436
  8.7 10.1 %copy-start.3 = (bf16[2048,64]{1,0:T(8,128)(2,1)S(1)}, bf16[2048,64]{1,0:T(8,128)(2,1)}, u32[]{:S(2)}) copy-start(bf16[2048,64]{1,0:T(8,128)(2,1)} %copy.17) | copy-start | bytes 786436
  8.7 10.1 %copy-start.5 = (bf16[256,2048]{1,0:T(8,128)(2,1)S(1)}, bf16[256,2048]{1,0:T(8,128)(2,1)}, u32[]{:S(2)}) copy-start(bf16[256,2048]{1,0:T(8,128)(2,1)} %param.12) | copy-start | bytes 3145732
  66.6 0.7 copy-start.8
  137.6 2.0 copy-start.6
  139.6 2.5 %copy-start.1 = (f32[64,10880]{0,1:T(8,128)}, f32[64,10880]{0,1:T(8,128)S(1)}, u32[]{:S(2)}) copy-start(f32[64,10880]{0,1:T(8,128)S(1)} %convert_element_type.36) | copy-start | bytes 8355844
  139.7 2.4 %copy-start.7 = (bf16[3584,64]{0,1:T(8,128)(2,1)S(1)}, bf16[3584,64]{0,1:T(8,128)(2,1)}, u32[]{:S(2)}) copy-start(bf16[3584,64]{0,1:T(8,128)(2,1)} %param.18) | copy-start | bytes 1376260
Sparse Core Ops, SparseCore 0:
  66.7 66.8 reduce-scatter.3
